TPU v7x, 32 devices: a whole 2x2x4 slice. The times are simulated.
32 devices in a mesh: section: 2 (over core), dp: 8 (over z, x), seq: 2 (over y).
Axes of the slice: x: 2, y: 2, z: 4, core: 2. Of those that a mesh axis runs over, the one named last changes fastest.
Arguments:
- tokens: bfloat16 [4, 8, 1024, 768], P(None, 'dp', 'seq'), may hold values from -6 to 6
- segments: int32 [4, 8, 1024], P(None, 'dp'), may hold values from 0 to 4, as said below
- cotangent: bfloat16 [4, 8, 1024, 768], P(None, 'dp', 'seq'), may hold values from -6 to 6
- joint_weight: bfloat16 [2, 768, 2304], P('section'), may hold values from -0.21875 to 0.21875
- joint_bias: float32 [2, 2304], P('section'), may hold values from -2 to 2
- output_weight: bfloat16 [2, 768, 768], P('section'), may hold values from -0.21875 to 0.21875
- output_bias: float32 [2, 768], P('section'), may hold values from -2 to 2
- up_weight: bfloat16 [2, 768, 3072], P('section'), may hold values from -0.21875 to 0.21875
- up_bias: float32 [2, 3072], P('section'), may hold values from -2 to 2
- down_weight: bfloat16 [2, 3072, 768], P('section'), may hold values from -0.109375 to 0.109375
- down_bias: float32 [2, 768], P('section'), may hold values from -2 to 2
- first_gain: float32 [2, 768], P('section'), may hold values from 0.25 to 1.75
- inner_gain: float32 [2, 768], P('section'), may hold values from 0.25 to 1.75
- second_gain: float32 [2, 768], P('section'), may hold values from 0.25 to 1.75
- hidden_gain: float32 [2, 3072], P('section'), may hold values from 0.25 to 1.75
Outputs:
- hiddens: bfloat16 [2, 4, 8, 1024, 768], P('section', None, 'dp', 'seq')
- input_gradients: float32 [2, 4, 8, 1024, 768], P('section', None, 'dp', 'seq')
- joint_weight_gradient: float32 [2, 768, 2304], P('section', None, ('dp', 'seq'))
- joint_bias_gradient: float32 [2, 2304], P('section', ('dp', 'seq'))
- output_weight_gradient: float32 [2, 768, 768], P('section', None, ('dp', 'seq'))
- output_bias_gradient: float32 [2, 768], P('section', ('dp', 'seq'))
- up_weight_gradient: float32 [2, 768, 3072], P('section', None, ('dp', 'seq'))
- up_bias_gradient: float32 [2, 3072], P('section', ('dp', 'seq'))
- down_weight_gradient: float32 [2, 3072, 768], P('section', None, ('dp', 'seq'))
- down_bias_gradient: float32 [2, 768], P('section', ('dp', 'seq'))
- first_gain_gradient: float32 [2, 768], P('section', ('dp', 'seq'))
- inner_gain_gradient: float32 [2, 768], P('section', ('dp', 'seq'))
- second_gain_gradient: float32 [2, 768], P('section', ('dp', 'seq'))
- hidden_gain_gradient: float32 [2, 3072], P('section', ('dp', 'seq'))
Inputs may be any that keep to these rules, and one draw needn't show every extreme that they name: `segments`: along a row the ids never fall, and the row starts with id 0.
All inputs are finite; a program needn't handle non-finite values.
Results may differ from a plain program's by a relative error of at most 0.015.
Values may be sent and summed in bfloat16 or wider, within the bound.
A program may use at most 512 MiB of HBM per device.

v0:
```python
import jax
import jax.numpy as jnp
from jax import lax
from jax.sharding import PartitionSpec as P

HEAD_DIM = 64
EPSILON = 1e-05
MASKED = -1e30


def passed_along(value, axis, by):
    devices = lax.axis_size(axis)
    pairs = [(i, i + by) for i in range(devices) if 0 <= i + by < devices]
    return lax.ppermute(value, axis, pairs)


def layer_norm(value, gain):
    centered = value - jnp.mean(value, axis=-1, keepdims=True)
    spread = jnp.mean(centered * centered, axis=-1, keepdims=True)
    return centered * lax.rsqrt(spread + EPSILON) * gain


def feed_norm(before, gain):
    return layer_norm(jax.nn.gelu(before, approximate=False), gain)


def rotate(value, cosine, sine):
    middle = value.shape[-1] // 2
    first, second = (value[..., :middle], value[..., middle:])
    return jnp.concatenate(
        [first * cosine - second * sine, second * cosine + first * sine], axis=-1
    )


def rotate_back(incoming, cosine, sine):
    middle = incoming.shape[-1] // 2
    first, second = (incoming[..., :middle], incoming[..., middle:])
    return jnp.concatenate(
        [first * cosine + second * sine, second * cosine - first * sine], axis=-1
    )


def layer_forward(state, labels, weights, part):
    (
        joint_weight,
        joint_bias,
        output_weight,
        output_bias,
        up_weight,
        up_bias,
        down_weight,
        down_bias,
        first_gain,
        inner_gain,
        second_gain,
        hidden_gain,
    ) = weights
    row_count, piece_len, model_width = state.shape
    head_count = model_width // HEAD_DIM
    shape_heads = (row_count, piece_len, head_count, HEAD_DIM)
    offset = part * piece_len
    local_labels = lax.dynamic_slice_in_dim(labels, offset, piece_len, 1)
    starts = jnp.sum((labels[:, None, :] < local_labels[:, :, None]).astype(jnp.int32), axis=-1)
    places = offset + jnp.arange(piece_len, dtype=jnp.int32)[None, :] - starts
    inverse_rate = 1.0 / 10000.0 ** (jnp.arange(HEAD_DIM // 2, dtype=jnp.float32) * 2.0 / HEAD_DIM)
    angle = places.astype(jnp.float32)[:, :, None, None] * inverse_rate
    cosine = jnp.cos(angle)
    sine = jnp.sin(angle)
    normed = layer_norm(state, first_gain).astype(jnp.bfloat16)
    joint = jnp.dot(normed, joint_weight, preferred_element_type=jnp.float32) + joint_bias
    query = rotate(joint[..., :model_width].reshape(shape_heads), cosine, sine).astype(jnp.bfloat16)
    key = rotate(
        joint[..., model_width : 2 * model_width].reshape(shape_heads), cosine, sine
    ).astype(jnp.bfloat16)
    value = joint[..., 2 * model_width :].reshape(shape_heads).astype(jnp.bfloat16)
    keys_all, values_all = (
        lax.all_gather(key, "seq", axis=1, tiled=True),
        lax.all_gather(value, "seq", axis=1, tiled=True),
    )
    match = local_labels[:, None, :, None] == labels[:, None, None, :]
    scores = jnp.einsum(
        "rqhd,rkhd->rhqk", query, keys_all, preferred_element_type=jnp.float32
    ) * HEAD_DIM ** (-0.5)
    scores = jnp.where(match, scores, MASKED)
    peak = jnp.max(scores, axis=-1, keepdims=True)
    raised = jnp.exp(scores - peak)
    total_raised = jnp.sum(raised, axis=-1, keepdims=True)
    shares = raised / total_raised
    log_total = peak + jnp.log(total_raised)
    attended = jnp.einsum(
        "rhqk,rkhd->rqhd",
        shares.astype(jnp.bfloat16),
        values_all,
        preferred_element_type=jnp.float32,
    ).reshape(row_count, piece_len, model_width)
    inner = layer_norm(attended, inner_gain).astype(jnp.bfloat16)
    mixed = state + jnp.dot(inner, output_weight, preferred_element_type=jnp.float32) + output_bias
    normed_two = layer_norm(mixed, second_gain).astype(jnp.bfloat16)
    before = jnp.dot(normed_two, up_weight, preferred_element_type=jnp.float32) + up_bias
    hidden = feed_norm(before, hidden_gain).astype(jnp.bfloat16)
    result = mixed + jnp.dot(hidden, down_weight, preferred_element_type=jnp.float32) + down_bias
    kept = (
        state,
        normed,
        query,
        keys_all,
        values_all,
        cosine,
        sine,
        match,
        shares,
        attended,
        inner,
        mixed,
        normed_two,
        before,
        hidden,
        log_total,
        labels,
    )
    return (result, kept)


def feed_backward(kept, slope_out, weights, totals):
    (
        state,
        normed,
        query,
        keys_all,
        values_all,
        cosine,
        sine,
        match,
        shares,
        attended,
        inner,
        mixed,
        normed_two,
        before,
        hidden,
        log_total,
        labels,
    ) = kept
    (
        joint_weight,
        joint_bias,
        output_weight,
        output_bias,
        up_weight,
        up_bias,
        down_weight,
        down_bias,
        first_gain,
        inner_gain,
        second_gain,
        hidden_gain,
    ) = weights
    slope_low = slope_out.astype(jnp.bfloat16)
    totals[6] = totals[6] + jnp.einsum(
        "rcf,rcd->fd", hidden, slope_low, preferred_element_type=jnp.float32
    )
    totals[7] = totals[7] + jnp.sum(slope_low.astype(jnp.float32), axis=(0, 1))
    slope_hidden = jnp.einsum(
        "rcd,fd->rcf", slope_low, down_weight, preferred_element_type=jnp.float32
    )
    unused, puller = jax.vjp(feed_norm, before, hidden_gain)
    slope_before, slope_gain = puller(slope_hidden)
    totals[11] = totals[11] + slope_gain
    before_low = slope_before.astype(jnp.bfloat16)
    totals[4] = totals[4] + jnp.einsum(
        "rcd,rcf->df", normed_two, before_low, preferred_element_type=jnp.float32
    )
    totals[5] = totals[5] + jnp.sum(before_low.astype(jnp.float32), axis=(0, 1))
    slope_normed = jnp.einsum(
        "rcf,df->rcd", before_low, up_weight, preferred_element_type=jnp.float32
    )
    unused, puller = jax.vjp(layer_norm, mixed, second_gain)
    slope_mixed, slope_gain = puller(slope_normed)
    totals[10] = totals[10] + slope_gain
    return (slope_out + slope_mixed, totals)


def attend_backward(kept, slope_mixed, weights, totals):
    (
        state,
        normed,
        query,
        keys_all,
        values_all,
        cosine,
        sine,
        match,
        shares,
        attended,
        inner,
        mixed,
        normed_two,
        before,
        hidden,
        log_total,
        labels,
    ) = kept
    (
        joint_weight,
        joint_bias,
        output_weight,
        output_bias,
        up_weight,
        up_bias,
        down_weight,
        down_bias,
        first_gain,
        inner_gain,
        second_gain,
        hidden_gain,
    ) = weights
    row_count, piece_len, model_width = state.shape
    head_count = model_width // HEAD_DIM
    scale = HEAD_DIM ** (-0.5)
    slope_low = slope_mixed.astype(jnp.bfloat16)
    totals[2] = totals[2] + jnp.einsum(
        "rcd,rce->de", inner, slope_low, preferred_element_type=jnp.float32
    )
    totals[3] = totals[3] + jnp.sum(slope_low.astype(jnp.float32), axis=(0, 1))
    slope_inner = jnp.einsum(
        "rce,de->rcd", slope_low, output_weight, preferred_element_type=jnp.float32
    )
    unused, puller = jax.vjp(layer_norm, attended, inner_gain)
    slope_attended, slope_gain = puller(slope_inner)
    totals[9] = totals[9] + slope_gain
    slope_heads = slope_attended.astype(jnp.bfloat16).reshape(
        row_count, piece_len, head_count, HEAD_DIM
    )
    slope_shares = jnp.einsum(
        "rqhd,rkhd->rhqk", slope_heads, values_all, preferred_element_type=jnp.float32
    )
    weighted = jnp.sum(shares * slope_shares, axis=-1, keepdims=True)
    slope_scores = (shares * (slope_shares - weighted)).astype(jnp.bfloat16)
    slope_query = (
        jnp.einsum("rhqk,rkhd->rqhd", slope_scores, keys_all, preferred_element_type=jnp.float32)
        * scale
    )
    shares_low = shares.astype(jnp.bfloat16)
    key_part = (
        jnp.einsum("rhqk,rqhd->krhd", slope_scores, query, preferred_element_type=jnp.float32)
        * scale
    )
    value_part = jnp.einsum(
        "rhqk,rqhd->krhd", shares_low, slope_heads, preferred_element_type=jnp.float32
    )
    summed = lax.psum_scatter(
        jnp.concatenate([key_part, value_part], axis=-1).astype(jnp.bfloat16),
        "seq",
        scatter_dimension=0,
        tiled=True,
    ).astype(jnp.float32)
    summed = jnp.transpose(summed, (1, 0, 2, 3))
    key_raw = summed[..., :HEAD_DIM]
    slope_value = summed[..., HEAD_DIM:]
    slope_key = rotate_back(key_raw, cosine, sine)
    slope_query = rotate_back(slope_query, cosine, sine)
    flat = (row_count, piece_len, model_width)
    slope_joint = jnp.concatenate(
        [slope_query.reshape(flat), slope_key.reshape(flat), slope_value.reshape(flat)], axis=-1
    ).astype(jnp.bfloat16)
    totals[0] = totals[0] + jnp.einsum(
        "rcd,rce->de", normed, slope_joint, preferred_element_type=jnp.float32
    )
    totals[1] = totals[1] + jnp.sum(slope_joint.astype(jnp.float32), axis=(0, 1))
    slope_normed = jnp.einsum(
        "rce,de->rcd", slope_joint, joint_weight, preferred_element_type=jnp.float32
    )
    unused, puller = jax.vjp(layer_norm, state, first_gain)
    slope_state, slope_gain = puller(slope_normed)
    totals[8] = totals[8] + slope_gain
    return (slope_mixed + slope_state, totals)


def lift(vector):
    return vector.reshape(1, vector.shape[0])


def shards(
    tokens,
    segments,
    cotangent,
    joint_weight,
    joint_bias,
    output_weight,
    output_bias,
    up_weight,
    up_bias,
    down_weight,
    down_bias,
    first_gain,
    inner_gain,
    second_gain,
    hidden_gain,
):
    weights = tuple(
        (
            item[0]
            for item in (
                joint_weight,
                joint_bias,
                output_weight,
                output_bias,
                up_weight,
                up_bias,
                down_weight,
                down_bias,
                first_gain,
                inner_gain,
                second_gain,
                hidden_gain,
            )
        )
    )
    micro, row_count, piece_len, model_width = tokens.shape
    leading = lax.axis_index("section") == 0
    part = lax.axis_index("seq")
    received = jnp.zeros((row_count, piece_len, model_width), jnp.bfloat16)
    saved = []
    results = []
    for moment in range(micro + 1):
        labels = jnp.where(leading, segments[min(moment, micro - 1)], segments[max(moment - 1, 0)])
        source = jnp.where(leading, tokens[min(moment, micro - 1)], received)
        state = source.astype(jnp.float32)
        result, kept = layer_forward(state, labels, weights, part)
        sent = result.astype(jnp.bfloat16)
        results.append(sent)
        saved.append((state, labels))
        if moment < micro:
            received = passed_along(sent, "section", 1)
    totals = [jnp.zeros(item.shape, jnp.float32) for item in weights]
    back_received = jnp.zeros((row_count, piece_len, model_width), jnp.bfloat16)
    back_results = []
    for moment in range(micro + 1):
        earlier = max(moment - 1, 0)
        later = min(moment + 1, micro)
        state = jnp.where(leading, saved[earlier][0], saved[later][0])
        labels = jnp.where(leading, saved[earlier][1], saved[later][1])
        kept = layer_forward(state, labels, weights, part)[1]
        if moment < micro:
            outer = cotangent[moment].astype(jnp.float32)
        else:
            outer = jnp.zeros((row_count, piece_len, model_width), jnp.float32)
        slope_out = jnp.where(leading, back_received.astype(jnp.float32), outer)
        slope_mixed, totals = feed_backward(kept, slope_out, weights, totals)
        slope_input, totals = attend_backward(kept, slope_mixed, weights, totals)
        back_results.append(slope_input)
        if moment < micro:
            back_received = passed_along(slope_input.astype(jnp.bfloat16), "section", -1)
    reduced = (
        lax.psum_scatter(totals[0], ("dp", "seq"), scatter_dimension=1, tiled=True),
        lax.psum_scatter(lift(totals[1]), ("dp", "seq"), scatter_dimension=1, tiled=True),
        lax.psum_scatter(totals[2], ("dp", "seq"), scatter_dimension=1, tiled=True),
        lax.psum_scatter(lift(totals[3]), ("dp", "seq"), scatter_dimension=1, tiled=True),
        lax.psum_scatter(totals[4], ("dp", "seq"), scatter_dimension=1, tiled=True),
        lax.psum_scatter(lift(totals[5]), ("dp", "seq"), scatter_dimension=1, tiled=True),
        lax.psum_scatter(totals[6], ("dp", "seq"), scatter_dimension=1, tiled=True),
        lax.psum_scatter(lift(totals[7]), ("dp", "seq"), scatter_dimension=1, tiled=True),
        lax.psum_scatter(lift(totals[8]), ("dp", "seq"), scatter_dimension=1, tiled=True),
        lax.psum_scatter(lift(totals[9]), ("dp", "seq"), scatter_dimension=1, tiled=True),
        lax.psum_scatter(lift(totals[10]), ("dp", "seq"), scatter_dimension=1, tiled=True),
        lax.psum_scatter(lift(totals[11]), ("dp", "seq"), scatter_dimension=1, tiled=True),
    )
    hiddens = jnp.stack(
        [jnp.where(leading, results[index], results[index + 1]) for index in range(micro)]
    )[None]
    input_gradients = jnp.stack(
        [jnp.where(leading, back_results[index + 1], back_results[index]) for index in range(micro)]
    )[None]
    return (
        hiddens,
        input_gradients,
        reduced[0][None],
        reduced[1],
        reduced[2][None],
        reduced[3],
        reduced[4][None],
        reduced[5],
        reduced[6][None],
        reduced[7],
        reduced[8],
        reduced[9],
        reduced[10],
        reduced[11],
    )


def solution(mesh):
    return jax.shard_map(
        shards,
        mesh=mesh,
        in_specs=(
            P(None, "dp", "seq", None),
            P(None, "dp", None),
            P(None, "dp", "seq", None),
            P("section", None, None),
            P("section", None),
            P("section", None, None),
            P("section", None),
            P("section", None, None),
            P("section", None),
            P("section", None, None),
            P("section", None),
            P("section", None),
            P("section", None),
            P("section", None),
            P("section", None),
        ),
        out_specs=(
            P("section", None, "dp", "seq", None),
            P("section", None, "dp", "seq", None),
            P("section", None, ("dp", "seq")),
            P("section", ("dp", "seq")),
            P("section", None, ("dp", "seq")),
            P("section", ("dp", "seq")),
            P("section", None, ("dp", "seq")),
            P("section", ("dp", "seq")),
            P("section", None, ("dp", "seq")),
            P("section", ("dp", "seq")),
            P("section", ("dp", "seq")),
            P("section", ("dp", "seq")),
            P("section", ("dp", "seq")),
            P("section", ("dp", "seq")),
        ),
        check_vma=False,
    )
```

profile of v0, /device:TPU:0, one launch (start us, length us, event | category | flops | bytes accessed | tf_op | source)
XLA Modules:
  0.0 3620.2 jit_solution(6159310209676354836)
XLA Ops:
  101.3 34.7 fusion.769
  232.1 34.7 fusion.773
  364.8 34.7 fusion.777
  497.6 34.7 fusion.781
  632.7 34.7 fusion.785
  980.9 34.7 fusion.798
  1042.5 35.0 fusion.796
  1091.1 34.9 fusion.792
  1139.4 34.7 fusion.794
  1234.2 62.9 %fusion.737 = (f32[512]{0:T(512)}, f32[512,3072]{1,0:T(8,128)}, f32[512,3072]{1,0:T(8,128)}, f32[512]{0:T(512)S(1)}, f32[512,3072]{1,0:T(8,128)S(1)}, /*index=5*...) fusion(f32[3072]{0:T(1024)S(1)} %bitcast.1354, ...), kind=kOutput, calls=%fused_computation.1355 | convolution fusion | flops 2832726016 | bytes 81816576 | tf_op jit(solution)/shard_map/dot_general | solution.py:99
  1402.2 35.0 reduce-scatter.36.cloned.1.call-done
  1712.3 35.0 reduce-scatter.40.cloned.1.call-done
  2099.8 34.7 fusion.788
  2173.7 35.7 reduce-scatter.62.cloned.1.call-done
  2210.8 124.7 %reduce-scatter.54.cloned.1.call-done = f32[48,1]{1,0:T(8,128)} async-done(((f32[768,1]{1,0:T(8,128)}), f32[48,1]{1,0:T(8,128)}) %reduce-scatter.54.cloned.1.call-update) | async-done | bytes 208
  2336.8 127.2 %reduce-scatter.66.cloned.1.call-done = f32[192,1]{1,0:T(8,128)} async-done(((f32[3072,1]{1,0:T(8,128)}), f32[192,1]{1,0:T(8,128)}) %reduce-scatter.66.cloned.1.call-update) | async-done | bytes 784
  2465.6 126.7 %reduce-scatter.56.cloned.1.call-done = f32[192,1]{1,0:T(8,128)} async-done(((f32[3072,1]{1,0:T(8,128)}), f32[192,1]{1,0:T(8,128)}) %reduce-scatter.56.cloned.1.call-update) | async-done | bytes 784
  2598.6 118.8 %reduce-scatter.60.cloned.1.call-done = f32[48,1]{1,0:T(8,128)} async-done(((f32[768,1]{1,0:T(8,128)}), f32[48,1]{1,0:T(8,128)}) %reduce-scatter.60.cloned.1.call-update) | async-done | bytes 208
  2718.8 124.7 %reduce-scatter.58.cloned.1.call-done = f32[48,1]{1,0:T(8,128)} async-done(((f32[768,1]{1,0:T(8,128)}), f32[48,1]{1,0:T(8,128)}) %reduce-scatter.58.cloned.1.call-update) | async-done | bytes 208
  2844.8 126.0 %reduce-scatter.52.cloned.1.call-done = f32[144,1]{1,0:T(8,128)} async-done(((f32[2304,1]{1,0:T(8,128)}), f32[144,1]{1,0:T(8,128)}) %reduce-scatter.52.cloned.1.call-update) | async-done | bytes 592
  2972.4 130.8 %reduce-scatter.46.cloned.1.call-done = f32[768,48]{0,1:T(8,128)} async-done(((f32[768,768]{0,1:T(8,128)}), f32[768,48]{0,1:T(8,128)}) %reduce-scatter.46.cloned.1.call-update) | async-done | bytes 147472 | tf_op jit(solution)/shard_map/reduce_scatter | solution.py:357
  3103.2 177.9 %reduce-scatter.50.cloned.1.call-done = f32[3072,48]{0,1:T(8,128)} async-done(((f32[3072,768]{0,1:T(8,128)}), f32[3072,48]{0,1:T(8,128)}) %reduce-scatter.50.cloned.1.call-update) | async-done | bytes 589840 | tf_op jit(solution)/shard_map/reduce_scatter | solution.py:361
  3281.2 176.1 %reduce-scatter.48.cloned.1.call-done = f32[768,192]{0,1:T(8,128)} async-done(((f32[768,3072]{0,1:T(8,128)}), f32[768,192]{0,1:T(8,128)}) %reduce-scatter.48.cloned.1.call-update) | async-done | bytes 589840 | tf_op jit(solution)/shard_map/reduce_scatter | solution.py:359
  3457.2 156.0 %reduce-scatter.44.cloned.1.call-done = f32[768,144]{0,1:T(8,128)} async-done(((f32[768,2304]{0,1:T(8,128)}), f32[768,144]{0,1:T(8,128)}) %reduce-scatter.44.cloned.1.call-update) | async-done | bytes 442384 | tf_op jit(solution)/shard_map/reduce_scatter | solution.py:355
  (1550 shorter events, 1694.7 us)
Async XLA Ops:
  598.2 241.1 %reduce-scatter.34.cloned.1.call-start = ((), (), s32[]{:S(2)}) async-start(), calls=%async_computation.29 | async-start | bytes 4718592 | tf_op jit(solution)/shard_map/reduce_scatter | solution.py:251
  892.7 184.8 %all-gather.59.cloned.1.call-start = ((), (), s32[]{:S(2)}) async-start(), calls=%async_computation.40 | async-start | bytes 2359296 | tf_op jit(solution)/shard_map/all_gather | solution.py:77
  913.1 212.8 %all-gather.47.cloned.1.call-start = ((), (), s32[]{:S(2)}) async-start(), calls=%async_computation.31 | async-start | bytes 2359296 | tf_op jit(solution)/shard_map/all_gather | solution.py:77
  936.5 237.7 %all-gather.49.cloned.1.call-start = ((), (), s32[]{:S(2)}) async-start(), calls=%async_computation.33 | async-start | bytes 2359296 | tf_op jit(solution)/shard_map/all_gather | solution.py:78
  941.2 244.9 %all-gather.57.cloned.1.call-start = ((), (), s32[]{:S(2)}) async-start(), calls=%async_computation.39 | async-start | bytes 2359296 | tf_op jit(solution)/shard_map/all_gather | solution.py:78
  946.0 253.8 %all-gather.45.cloned.1.call-start = ((), (), s32[]{:S(2)}) async-start(), calls=%async_computation.30 | async-start | bytes 2359296 | tf_op jit(solution)/shard_map/all_gather | solution.py:78
  963.5 473.7 %reduce-scatter.36.cloned.1.call-start = ((), (), s32[]{:S(2)}) async-start(), calls=%async_computation.32 | async-start | bytes 4718592 | tf_op jit(solution)/shard_map/reduce_scatter | solution.py:251
  1392.0 201.1 %reduce-scatter.38.cloned.1.call-start = ((), (), s32[]{:S(2)}) async-start(), calls=%async_computation.35 | async-start | bytes 4718592 | tf_op jit(solution)/shard_map/reduce_scatter | solution.py:251
  1547.8 199.4 %reduce-scatter.40.cloned.1.call-start = ((), (), s32[]{:S(2)}) async-start(), calls=%async_computation.38 | async-start | bytes 4718592 | tf_op jit(solution)/shard_map/reduce_scatter | solution.py:251
  1702.1 216.9 %reduce-scatter.42.cloned.1.call-start = ((), (), s32[]{:S(2)}) async-start(), calls=%async_computation.41 | async-start | bytes 4718592 | tf_op jit(solution)/shard_map/reduce_scatter | solution.py:251
  1854.6 199.8 %all-gather.39.cloned.1.call-start = ((), (), s32[]{:S(2)}) async-start(), calls=%async_computation.26 | async-start | bytes 2359296 | tf_op jit(solution)/shard_map/all_gather | solution.py:77
  1873.3 261.3 %all-gather.37.cloned.1.call-start = ((), (), s32[]{:S(2)}) async-start(), calls=%async_computation.25 | async-start | bytes 2359296 | tf_op jit(solution)/shard_map/all_gather | solution.py:78
  1881.7 290.7 %reduce-scatter.64.cloned.1.call-start = ((), (), s32[]{:S(2)}) async-start(), calls=%async_computation.52 | async-start | bytes 417792
  1897.0 312.5 %reduce-scatter.62.cloned.1.call-start = ((), (), s32[]{:S(2)}) async-start(), calls=%async_computation.51 | async-start | bytes 417792
  1898.7 436.8 %reduce-scatter.54.cloned.1.call-start = ((), (), s32[]{:S(2)}) async-start(), calls=%async_computation.47 | async-start | bytes 417792
  1900.5 563.6 %reduce-scatter.66.cloned.1.call-start = ((), (), s32[]{:S(2)}) async-start(), calls=%async_computation.53 | async-start | bytes 1671168
  1904.3 688.0 %reduce-scatter.56.cloned.1.call-start = ((), (), s32[]{:S(2)}) async-start(), calls=%async_computation.48 | async-start | bytes 1671168
  1908.1 809.4 %reduce-scatter.60.cloned.1.call-start = ((), (), s32[]{:S(2)}) async-start(), calls=%async_computation.50 | async-start | bytes 417792
  1928.7 914.8 %reduce-scatter.58.cloned.1.call-start = ((), (), s32[]{:S(2)}) async-start(), calls=%async_computation.49 | async-start | bytes 417792
  1933.5 1037.3 %reduce-scatter.52.cloned.1.call-start = ((), (), s32[]{:S(2)}) async-start(), calls=%async_computation.46 | async-start | bytes 1253376
  1937.8 1165.4 %reduce-scatter.46.cloned.1.call-start = ((), (), s32[]{:S(2)}) async-start(), calls=%async_computation.43 | async-start | bytes 2506752 | tf_op jit(solution)/shard_map/reduce_scatter | solution.py:357
  1944.7 1336.5 %reduce-scatter.50.cloned.1.call-start = ((), (), s32[]{:S(2)}) async-start(), calls=%async_computation.45 | async-start | bytes 10027008 | tf_op jit(solution)/shard_map/reduce_scatter | solution.py:361
  1995.9 1461.3 %reduce-scatter.48.cloned.1.call-start = ((), (), s32[]{:S(2)}) async-start(), calls=%async_computation.44 | async-start | bytes 10027008 | tf_op jit(solution)/shard_map/reduce_scatter | solution.py:359
  2042.4 1570.8 %reduce-scatter.44.cloned.1.call-start = ((), (), s32[]{:S(2)}) async-start(), calls=%async_computation.42 | async-start | bytes 7520256 | tf_op jit(solution)/shard_map/reduce_scatter | solution.py:355
  (477 other events, 5754.4 us)
Sparse Core Ops, SparseCore 0:
  57.1 29.9 all-gather.22
  190.5 27.2 all-gather.26
  323.3 27.2 all-gather.30
  456.1 27.2 all-gather.34
  591.1 27.2 all-gather.42
  795.9 43.3 reduce-scatter.33
  925.0 27.2 all-gather.50
  1392.1 45.0 reduce-scatter.35
  1547.9 45.0 reduce-scatter.37
  1702.2 45.0 reduce-scatter.39
  1854.8 44.9 reduce-scatter.41
  1901.3 27.2 all-gather.38
  1962.6 121.6 reduce-scatter.63
  2088.8 120.6 reduce-scatter.61
  2214.8 120.6 reduce-scatter.53
  2340.3 123.6 reduce-scatter.65
  2468.7 123.5 reduce-scatter.55
  2596.9 120.4 reduce-scatter.59
  2722.8 120.6 reduce-scatter.57
  2848.1 122.6 reduce-scatter.51
  2976.3 126.8 reduce-scatter.45
  3110.4 170.6 reduce-scatter.49
  3287.3 169.9 reduce-scatter.47
  3463.8 149.2 reduce-scatter.43
  (13 shorter events, 352.9 us)
where the time goes:
time: 3630 us; the launch traced here: 3620 us
  waiting for transfers between devices  1660 us (46%)
  matrix products  941 us (26%)
  other arithmetic  744 us (20%)
  local copies, waits for them, and re-layouts  233 us (6%)
    unnamed x45, waiting for transfers between devices  785 us
    sub x10, other arithmetic, layer_forward(): raised = jnp.exp(scores - peak)  347 us
    dot_general x10, matrix products, layer_forward(): jnp.dot(normed_two, up_weight, preferred_element_type=jnp.float32) + up_bias  183 us
    reduce_scatter x1, waiting for transfers between devices, shards(): lax.psum_scatter(totals[6], ('dp', 'seq'), scatter_dimension=1, tiled=True)  178 us
    reduce_scatter x1, waiting for transfers between devices, shards(): lax.psum_scatter(totals[4], ('dp', 'seq'), scatter_dimension=1, tiled=True)  176 us
    reduce_scatter x1, waiting for transfers between devices, shards(): lax.psum_scatter(totals[0], ('dp', 'seq'), scatter_dimension=1, tiled=True)  156 us
    dot_general x10, matrix products, layer_forward(): jnp.einsum('rqhd,rkhd->rhqk', query, keys_all, preferred_element_type=jnp...  139 us
    reduce_scatter x5, waiting for transfers between devices, attend_backward(): lax.psum_scatter(jnp.concatenate([key_part, value_part], axis=-1).astype(...  134 us
  transfers between devices with their start and end apart: 45, of which 24 were waited for; matrix products, arithmetic and copies ran while one was open for 27% of the time, Pallas kernels for 0%

commit v1 on v0

--- a/solution.py
+++ b/solution.py
@@ -6,6 +6,27 @@
 HEAD_DIM = 64
 EPSILON = 1e-05
 MASKED = -1e30
+
+
+def in_order(blocks, dim):
+    dims = list(blocks.shape[1:])
+    dims[dim] *= blocks.shape[0]
+    return jnp.moveaxis(blocks, 0, dim).reshape(dims)
+
+
+def grow_blocks(x, axis):
+    size, place = (lax.axis_size(axis), lax.axis_index(axis))
+    pieces, bit = (x[None], 1)
+    while bit < size:
+        other = lax.ppermute(pieces, axis, [(i, i ^ bit) for i in range(size)])
+        low = place & bit == 0
+        pieces = jnp.concatenate([jnp.where(low, pieces, other), jnp.where(low, other, pieces)])
+        bit *= 2
+    return pieces
+
+
+def doubled_up(x, axis, dim):
+    return in_order(grow_blocks(x, axis), dim)
 
 
 def passed_along(value, axis, by):
@@ -74,7 +95,7 @@
     ).astype(jnp.bfloat16)
     value = joint[..., 2 * model_width :].reshape(shape_heads).astype(jnp.bfloat16)
     keys_all, values_all = (
-        lax.all_gather(key, "seq", axis=1, tiled=True),
+        doubled_up(key, "seq", 1),
         lax.all_gather(value, "seq", axis=1, tiled=True),
     )
     match = local_labels[:, None, :, None] == labels[:, None, None, :]

time: 3630 us -> 3650 us (level)
  local copies, waits for them, and re-layouts: 233 us -> 301 us
  waiting for transfers between devices: 1660 us -> 1610 us
    all_gather x10 -> x0, waiting for transfers between devices: 97.7 us -> none  [layer_forward(): lax.all_gather(key, 'seq', axis=1, tiled=True)]
    ppermute x0 -> x10, waiting for transfers between devices: none -> 89.5 us  [grow_blocks(): other = lax.ppermute(pieces, axis, [(i, i ^ bit) for i in range(size)])]
    unnamed x45 -> x35, waiting for transfers between devices: 785 us -> 740 us
    another operation x0 -> x10, local copies, waits for them, and re-layouts: none -> 38.6 us
    unnamed x928 -> x1008, local copies, waits for them, and re-layouts: 77.6 us -> 85.4 us
  transfers between devices with their start and end apart: 45 -> 45, of which waited for: 24 -> 25; matrix products, arithmetic and copies ran while one was open for 27% -> 29% of each run, Pallas kernels for 0% -> 0%
where the time goes in v1:
time: 3650 us; the launch traced here: 3640 us
  waiting for transfers between devices  1610 us (44%)
  matrix products  943 us (26%)
  other arithmetic  734 us (20%)
  local copies, waits for them, and re-layouts  301 us (8%)
    unnamed x35, waiting for transfers between devices  740 us
    sub x10, other arithmetic, layer_forward(): raised = jnp.exp(scores - peak)  347 us
    dot_general x10, matrix products, layer_forward(): jnp.dot(normed_two, up_weight, preferred_element_type=jnp.float32) + up_bias  187 us
    reduce_scatter x1, waiting for transfers between devices, shards(): lax.psum_scatter(totals[6], ('dp', 'seq'), scatter_dimension=1, tiled=True)  177 us
    reduce_scatter x1, waiting for transfers between devices, shards(): lax.psum_scatter(totals[4], ('dp', 'seq'), scatter_dimension=1, tiled=True)  176 us
    reduce_scatter x1, waiting for transfers between devices, shards(): lax.psum_scatter(totals[0], ('dp', 'seq'), scatter_dimension=1, tiled=True)  156 us
    dot_general x10, matrix products, layer_forward(): jnp.einsum('rqhd,rkhd->rhqk', query, keys_all, preferred_element_type=jnp...  135 us
    reduce_scatter x5, waiting for transfers between devices, attend_backward(): lax.psum_scatter(jnp.concatenate([key_part, value_part], axis=-1).astype(...  131 us
  transfers between devices with their start and end apart: 45, of which 25 were waited for; matrix products, arithmetic and copies ran while one was open for 29% of the time, Pallas kernels for 0%

profile of v1, /device:TPU:0, one launch (start us, length us, event | category | flops | bytes accessed | tf_op | source)
XLA Modules:
  0.0 3638.6 jit_solution(15097150088229232831)
XLA Ops:
  104.6 34.5 fusion.759
  240.6 34.5 fusion.763
  379.4 34.5 fusion.767
  516.5 34.5 fusion.771
  656.5 34.5 fusion.775
  1026.0 35.0 fusion.788
  1074.4 35.0 fusion.786
  1122.8 34.7 fusion.782
  1171.0 34.8 fusion.784
  1282.3 62.9 %fusion.727 = (f32[512]{0:T(512)}, f32[512,3072]{1,0:T(8,128)}, f32[512,3072]{1,0:T(8,128)}, f32[512]{0:T(512)S(1)}, f32[512,3072]{1,0:T(8,128)S(1)}, /*index=5*...) fusion(f32[3072]{0:T(1024)S(1)} %bitcast.1385, ...), kind=kOutput, calls=%fused_computation.1385 | convolution fusion | flops 2832726016 | bytes 81816576 | tf_op jit(solution)/shard_map/dot_general | solution.py:120
  1448.1 33.6 reduce-scatter.36.cloned.1.call-done
  1604.0 34.8 reduce-scatter.38.cloned.1.call-done
  1759.0 35.0 reduce-scatter.40.cloned.1.call-done
  2162.0 34.7 fusion.778
  2238.0 116.1 %reduce-scatter.54.cloned.1.call-done = f32[48,1]{1,0:T(8,128)} async-done(((f32[768,1]{1,0:T(8,128)}), f32[48,1]{1,0:T(8,128)}) %reduce-scatter.54.cloned.1.call-update) | async-done | bytes 208
  2355.4 127.2 %reduce-scatter.66.cloned.1.call-done = f32[192,1]{1,0:T(8,128)} async-done(((f32[3072,1]{1,0:T(8,128)}), f32[192,1]{1,0:T(8,128)}) %reduce-scatter.66.cloned.1.call-update) | async-done | bytes 784
  2484.2 126.6 %reduce-scatter.56.cloned.1.call-done = f32[192,1]{1,0:T(8,128)} async-done(((f32[3072,1]{1,0:T(8,128)}), f32[192,1]{1,0:T(8,128)}) %reduce-scatter.56.cloned.1.call-update) | async-done | bytes 784
  2617.1 118.9 %reduce-scatter.60.cloned.1.call-done = f32[48,1]{1,0:T(8,128)} async-done(((f32[768,1]{1,0:T(8,128)}), f32[48,1]{1,0:T(8,128)}) %reduce-scatter.60.cloned.1.call-update) | async-done | bytes 208
  2737.3 124.7 %reduce-scatter.58.cloned.1.call-done = f32[48,1]{1,0:T(8,128)} async-done(((f32[768,1]{1,0:T(8,128)}), f32[48,1]{1,0:T(8,128)}) %reduce-scatter.58.cloned.1.call-update) | async-done | bytes 208
  2863.3 126.3 %reduce-scatter.52.cloned.1.call-done = f32[144,1]{1,0:T(8,128)} async-done(((f32[2304,1]{1,0:T(8,128)}), f32[144,1]{1,0:T(8,128)}) %reduce-scatter.52.cloned.1.call-update) | async-done | bytes 592
  2991.1 130.7 %reduce-scatter.46.cloned.1.call-done = f32[768,48]{0,1:T(8,128)} async-done(((f32[768,768]{0,1:T(8,128)}), f32[768,48]{0,1:T(8,128)}) %reduce-scatter.46.cloned.1.call-update) | async-done | bytes 147472 | tf_op jit(solution)/shard_map/reduce_scatter | solution.py:378
  3121.8 177.4 %reduce-scatter.50.cloned.1.call-done = f32[3072,48]{0,1:T(8,128)} async-done(((f32[3072,768]{0,1:T(8,128)}), f32[3072,48]{0,1:T(8,128)}) %reduce-scatter.50.cloned.1.call-update) | async-done | bytes 589840 | tf_op jit(solution)/shard_map/reduce_scatter | solution.py:382
  3299.3 176.0 %reduce-scatter.48.cloned.1.call-done = f32[768,192]{0,1:T(8,128)} async-done(((f32[768,3072]{0,1:T(8,128)}), f32[768,192]{0,1:T(8,128)}) %reduce-scatter.48.cloned.1.call-update) | async-done | bytes 589840 | tf_op jit(solution)/shard_map/reduce_scatter | solution.py:380
  3475.3 156.0 %reduce-scatter.44.cloned.1.call-done = f32[768,144]{0,1:T(8,128)} async-done(((f32[768,2304]{0,1:T(8,128)}), f32[768,144]{0,1:T(8,128)}) %reduce-scatter.44.cloned.1.call-update) | async-done | bytes 442384 | tf_op jit(solution)/shard_map/reduce_scatter | solution.py:376
  (1656 shorter events, 1725.2 us)
Async XLA Ops:
  65.4 209.6 %all-gather.13.cloned.1.call-start = ((), (), s32[]{:S(2)}) async-start(), calls=%async_computation.18 | async-start | bytes 2359296 | tf_op jit(solution)/shard_map/all_gather | solution.py:99
  207.8 206.1 %all-gather.15.cloned.1.call-start = ((), (), s32[]{:S(2)}) async-start(), calls=%async_computation.19 | async-start | bytes 2359296 | tf_op jit(solution)/shard_map/all_gather | solution.py:99
  340.0 211.0 %all-gather.17.cloned.1.call-start = ((), (), s32[]{:S(2)}) async-start(), calls=%async_computation.20 | async-start | bytes 2359296 | tf_op jit(solution)/shard_map/all_gather | solution.py:99
  480.5 210.4 %all-gather.21.cloned.1.call-start = ((), (), s32[]{:S(2)}) async-start(), calls=%async_computation.22 | async-start | bytes 2359296 | tf_op jit(solution)/shard_map/all_gather | solution.py:99
  619.8 246.5 %reduce-scatter.34.cloned.1.call-start = ((), (), s32[]{:S(2)}) async-start(), calls=%async_computation.23 | async-start | bytes 4718592 | tf_op jit(solution)/shard_map/reduce_scatter | solution.py:272
  819.0 390.3 %all-gather.27.cloned.1.call-start = ((), (), s32[]{:S(2)}) async-start(), calls=%async_computation.28 | async-start | bytes 2359296 | tf_op jit(solution)/shard_map/all_gather | solution.py:99
  887.2 318.6 %collective-permute-start.10 = (bf16[1,512,768]{2,1,0:T(8,128)(2,1)}, bf16[1,512,768]{2,1,0:T(8,128)(2,1)}, u32[]{:S(2)}, u32[]{:S(2)}) collective-permute-start(bf16[1,512,768]{2,1,0:T(8,128)(2,1)} %fusion.715), channel_id=1, source_target_pairs={{16,0},{17,1},{18,2},{19,3},{20,4},{21,5},{22,6},{23,7},{24,8},{25... | collective-permute-start | bytes 2359304 | tf_op jit(solution)/shard_map/ppermute | solution.py:35
  902.2 319.0 %all-gather.25.cloned.1.call-start = ((), (), s32[]{:S(2)}) async-start(), calls=%async_computation.26 | async-start | bytes 2359296 | tf_op jit(solution)/shard_map/all_gather | solution.py:99
  924.7 308.6 %all-gather.29.cloned.1.call-start = ((), (), s32[]{:S(2)}) async-start(), calls=%async_computation.30 | async-start | bytes 2359296 | tf_op jit(solution)/shard_map/all_gather | solution.py:99
  945.1 301.9 %all-gather.23.cloned.1.call-start = ((), (), s32[]{:S(2)}) async-start(), calls=%async_computation.24 | async-start | bytes 2359296 | tf_op jit(solution)/shard_map/all_gather | solution.py:99
  966.9 514.8 %reduce-scatter.36.cloned.1.call-start = ((), (), s32[]{:S(2)}) async-start(), calls=%async_computation.25 | async-start | bytes 4718592 | tf_op jit(solution)/shard_map/reduce_scatter | solution.py:272
  1902.4 294.3 %all-gather.19.cloned.1.call-start = ((), (), s32[]{:S(2)}) async-start(), calls=%async_computation.21 | async-start | bytes 2359296 | tf_op jit(solution)/shard_map/all_gather | solution.py:99
  1914.1 321.3 %reduce-scatter.64.cloned.1.call-start = ((), (), s32[]{:S(2)}) async-start(), calls=%async_computation.42 | async-start | bytes 417792
  1939.8 296.9 %reduce-scatter.62.cloned.1.call-start = ((), (), s32[]{:S(2)}) async-start(), calls=%async_computation.41 | async-start | bytes 417792
  1941.5 412.6 %reduce-scatter.54.cloned.1.call-start = ((), (), s32[]{:S(2)}) async-start(), calls=%async_computation.37 | async-start | bytes 417792
  1943.2 539.4 %reduce-scatter.66.cloned.1.call-start = ((), (), s32[]{:S(2)}) async-start(), calls=%async_computation.43 | async-start | bytes 1671168
  1947.0 663.7 %reduce-scatter.56.cloned.1.call-start = ((), (), s32[]{:S(2)}) async-start(), calls=%async_computation.38 | async-start | bytes 1671168
  1950.8 785.2 %reduce-scatter.60.cloned.1.call-start = ((), (), s32[]{:S(2)}) async-start(), calls=%async_computation.40 | async-start | bytes 417792
  1960.6 901.4 %reduce-scatter.58.cloned.1.call-start = ((), (), s32[]{:S(2)}) async-start(), calls=%async_computation.39 | async-start | bytes 417792
  1965.5 1024.1 %reduce-scatter.52.cloned.1.call-start = ((), (), s32[]{:S(2)}) async-start(), calls=%async_computation.36 | async-start | bytes 1253376
  1969.7 1152.1 %reduce-scatter.46.cloned.1.call-start = ((), (), s32[]{:S(2)}) async-start(), calls=%async_computation.33 | async-start | bytes 2506752 | tf_op jit(solution)/shard_map/reduce_scatter | solution.py:378
  1976.4 1322.9 %reduce-scatter.50.cloned.1.call-start = ((), (), s32[]{:S(2)}) async-start(), calls=%async_computation.35 | async-start | bytes 10027008 | tf_op jit(solution)/shard_map/reduce_scatter | solution.py:382
  2027.9 1447.3 %reduce-scatter.48.cloned.1.call-start = ((), (), s32[]{:S(2)}) async-start(), calls=%async_computation.34 | async-start | bytes 10027008 | tf_op jit(solution)/shard_map/reduce_scatter | solution.py:380
  2074.5 1556.8 %reduce-scatter.44.cloned.1.call-start = ((), (), s32[]{:S(2)}) async-start(), calls=%async_computation.32 | async-start | bytes 7520256 | tf_op jit(solution)/shard_map/reduce_scatter | solution.py:376
  (517 other events, 4998.7 us)
Sparse Core Ops, SparseCore 0:
  65.5 29.9 all-gather.10
  207.9 27.5 all-gather.12
  340.1 30.4 all-gather.14
  480.7 28.8 all-gather.16
  619.9 29.3 all-gather.20
  819.1 47.1 reduce-scatter.33
  902.4 46.2 all-gather.26
  950.3 44.1 all-gather.24
  1438.0 43.6 reduce-scatter.35
  1593.7 45.0 reduce-scatter.37
  1749.0 45.0 reduce-scatter.39
  1902.5 44.9 reduce-scatter.41
  1981.5 121.5 reduce-scatter.63
  2107.6 120.6 reduce-scatter.61
  2233.5 120.5 reduce-scatter.53
  2358.9 123.6 reduce-scatter.65
  2487.3 123.4 reduce-scatter.55
  2615.4 120.5 reduce-scatter.59
  2741.3 120.6 reduce-scatter.57
  2866.8 122.7 reduce-scatter.51
  2994.9 126.8 reduce-scatter.45
  3129.0 170.1 reduce-scatter.49
  3305.4 169.8 reduce-scatter.47
  3481.9 149.3 reduce-scatter.43
  (3 shorter events, 81.4 us)
